TPU v7x, 512 devices: a whole 4x4x16 slice. The times are simulated.
512 devices in a mesh: voxel: 32 (over x, z_lo, core), feature: 4 (over z_hi), tm: 4 (over y).
Axes of the slice: x: 4, y: 4, z: 16 (z_hi: 4, z_lo: 4; z = z_hi * 4 + z_lo), core: 2. Of those that a mesh axis runs over, the one named last changes fastest.
Arguments:
- hidden: bfloat16 [3072, 8192], P('tm', 'feature'), may hold values from -6 to 6
- bold: bfloat16 [3072, 4096], P('tm', 'voxel'), may hold values from -6 to 6
- panel: bfloat16 [65536, 128], P(('feature', 'tm'), 'voxel'), may hold values from -0.0234375 to 0.0234375
- eigvals: float32 [128], replicated, may hold values from 0.05 to 2
- ridge_grid: int32 [24], replicated, may hold values from 0 to 16
- delays: int32 [8], replicated, may hold values from 1 to 12, as said below
- runs: int32 [3072], replicated, may hold values from 0 to 7, never falling along the last dimension, each value on 1 to 768 neighbouring positions
Outputs:
- scaled: bfloat16 [24, 128, 4096], P(None, None, 'voxel')
Inputs may be any that keep to these rules, and one draw needn't show every extreme that they name: 8 distinct delays, 12 among them. `runs`: run numbers never fall along the TRs; a run holds 1 to 768 TRs.
All inputs are finite; a program needn't handle non-finite values.
Results may differ from a plain program's by a relative error of at most 0.022.
Values may be sent and summed in bfloat16 or wider, within the bound.
A program may use at most 64 MiB of HBM per device.

v0:
```python
import math
import jax
import jax.numpy as jnp
from jax import lax
from jax.sharding import PartitionSpec as P

DELAYS = 8
MAXD = 12


def passed_along(value, axis, steps):
    count = lax.axis_size(axis)
    first, last = (max(0, -steps), min(count, count - steps))
    return lax.ppermute(value, axis, [(source, source + steps) for source in range(first, last)])


def contract_rows(left, right):
    return lax.dot_general(
        left, right, (((0,), (0,)), ((), ())), preferred_element_type=jnp.float32
    )


def shards(hidden, bold, panel, eigvals, ridge_grid, delays, runs):
    t_rows = hidden.shape[0]
    d_local = hidden.shape[1]
    v_cols = bold.shape[1]
    total_rows = t_rows * lax.axis_size("tm")
    first = lax.axis_index("tm") * t_rows
    ahead = passed_along(bold[:MAXD], "tm", -1)
    extended = jnp.concatenate([bold, ahead], 0)
    runs_pad = jnp.concatenate([runs, jnp.full((MAXD,), -1, jnp.int32)])
    own_runs = lax.dynamic_slice_in_dim(runs, first, t_rows)
    positions = first + jnp.arange(t_rows, dtype=jnp.int32)
    lagged_list = []
    for slot in range(DELAYS):
        offset = delays[slot]
        target_runs = lax.dynamic_slice_in_dim(runs_pad, first + offset, t_rows)
        valid = (positions + offset < total_rows) & (target_runs == own_runs)
        moved = lax.dynamic_slice_in_dim(extended, offset, t_rows, 0)
        lagged_list.append(jnp.where(valid[:, None], moved, jnp.zeros_like(moved)))
    stacked = jnp.stack(lagged_list, 1).reshape(t_rows, DELAYS * v_cols)
    cross = contract_rows(hidden, stacked)
    partial_cov = cross.reshape(d_local * DELAYS, v_cols).astype(jnp.bfloat16)
    panel_rows = lax.all_gather(panel, "tm", axis=0, tiled=True)
    rotated_part = contract_rows(
        lax.all_gather(panel_rows, "voxel", axis=1, tiled=True), partial_cov
    )
    rotated = lax.psum(rotated_part.astype(jnp.bfloat16), ("feature", "tm")).astype(jnp.float32)
    penalty = 2.0 ** ((ridge_grid.astype(jnp.float32) - 8.0) * 0.5)
    scaled = rotated[None] / (
        math.sqrt(total_rows) * (eigvals[None, :, None] + penalty[:, None, None])
    )
    return scaled.astype(jnp.bfloat16)


def solution(mesh):
    return jax.shard_map(
        shards,
        mesh=mesh,
        in_specs=(
            P("tm", "feature"),
            P("tm", "voxel"),
            P(("feature", "tm"), "voxel"),
            P(),
            P(),
            P(),
            P(),
        ),
        out_specs=P(None, None, "voxel"),
        check_vma=False,
    )
```

profile of v0, /device:TPU:2, one launch (start us, length us, event | category | flops | bytes accessed | tf_op | source)
XLA Modules:
  0.0 209.7 jit_solution(480760499588680285)
XLA Ops:
  6.5 14.4 %all_gather.6 = bf16[16384,4]{0,1:T(4,128)(2,1)} all-gather(bf16[4096,4]{0,1:T(4,128)(2,1)} %param.9), channel_id=1, replica_groups=mesh['voxel'=32,'feature'=4,'tm'=4] {'tm'}, dimensions={0}, use_global_device_ids=true | all-gather | bytes 163840 | tf_op jit(solution)/shard_map/all_gather | solution.py:44
  20.9 0.7 slice.28
  21.8 1.3 collective-permute-start
  23.1 1.6 fusion.49
  29.6 4.1 %fusion.48 = (pred[768]{0:T(1024)(128)(4,1)S(1)}, pred[768]{0:T(1024)(128)(4,1)S(1)}, pred[768]{0:T(1024)(128)(4,1)S(1)}, pred[768]{0:T(1024)(128)(4,1)S(1)}, pred[768]{0:T(1024)(128)(4,1)S(1)}) fusion(s32[]{:T(128)S(6)} %select_n.98, s32[3072]{0:T(1024)} %param.13, s32[]{:T(128)} %bitcast.14, s32[]{:T(128)S(6)} %mul.17, s32[]{:T(128)S(6)} %select_n.77, ...), kind=kLoop, calls=%fused_computation.77 | loop fusion | flops 16128 | bytes 22812 | tf_op jit(solution)/shard_map/and | solution.py:38
  33.7 0.7 multiply_power_fusion
  34.4 0.7 add_multiply_fusion
  35.1 2.7 %fusion.47 = (pred[768]{0:T(1024)(128)(4,1)S(1)}, pred[768]{0:T(1024)(128)(4,1)S(1)}, pred[768]{0:T(1024)(128)(4,1)S(1)}) fusion(s32[]{:T(128)S(6)} %select_n.95, s32[3072]{0:T(1024)} %param.13, s32[]{:T(128)} %bitcast.12, s32[]{:T(128)S(6)} %mul.17, s32[]{:T(128)S(6)} %select_n.77, s32[]{:T(128)S(6)} %select_n.80, s32[]{:T(128)} %bitcast.2, ...), kind=kLoop, calls=%fused_computation.76 | loop fusion | flops 9984 | bytes 20244 | tf_op jit(solution)/shard_map/and | solution.py:38
  38.5 1.1 copy.14
  53.9 0.2 fusion.12
  54.1 0.2 fusion.16
  54.3 0.2 fusion.20
  54.5 0.2 fusion.24
  54.7 0.2 fusion.28
  54.9 0.2 fusion.32
  55.1 0.2 fusion.4
  55.3 5.0 %convert_bitcast_fusion = bf16[2048,1024]{0,1:T(8,128)(2,1)} fusion(bf16[768,1024]{0,1:T(8,128)(2,1)S(1)} %bitcast.53, bf16[768,2048]{1,0:T(8,128)(2,1)S(1)} %copy-done), kind=kOutput, calls=%fused_computation | convolution fusion | flops 3223322624 | bytes 8912896 | tf_op jit(solution)/shard_map/dot_general | solution.py:18
  60.3 6.4 %copy.15 = bf16[2048,1024]{1,0:T(8,128)(2,1)} copy(bf16[2048,1024]{0,1:T(8,128)(2,1)} %convert_bitcast_fusion) | data formatting | bytes 8388608 | tf_op jit(solution)/shard_map/convert_element_type | solution.py:43
  66.7 7.4 %convert_element_type.26 = bf16[16384,128]{1,0:T(8,128)(2,1)} reshape(bf16[2048,1024]{1,0:T(8,128)(2,1)} %copy.15) | data formatting | bytes 8388608 | tf_op jit(solution)/shard_map/convert_element_type | solution.py:43
  74.1 17.7 %all-gather.3.cloned.1.call-done = bf16[32,4,16384]{2,1,0:T(4,128)(2,1)} async-done(((bf16[1,4,16384]{2,1,0:T(4,128)(2,1)}), bf16[32,4,16384]{2,1,0:T(4,128)(2,1)}) %all-gather.3.cloned.1.call-update) | async-done | bytes 4194320 | tf_op jit(solution)/shard_map/all_gather | solution.py:46
  91.8 6.9 %reshape.50 = bf16[128,16384]{1,0:T(8,128)(2,1)} reshape(bf16[32,4,16384]{2,1,0:T(4,128)(2,1)} %all-gather.3.cloned.1.call-done) | data formatting | bytes 8388608
  98.7 4.8 %fusion = bf16[128,128]{0,1:T(8,128)(2,1)S(1)} fusion(bf16[16384,128]{1,0:T(8,128)(2,1)} %convert_element_type.26, bf16[128,16384]{1,0:T(8,128)(2,1)} %reshape.50), kind=kOutput, calls=%fused_computation.3 | convolution fusion | flops 536887296 | bytes 8421376 | tf_op jit(solution)/shard_map/dot_general | solution.py:18
  103.5 97.9 %psum.7 = bf16[128,128]{0,1:T(8,128)(2,1)S(1)} all-reduce(bf16[128,128]{0,1:T(8,128)(2,1)S(1)} %fusion), channel_id=1, replica_groups=mesh['voxel'=32,'feature'=4,'tm'=4] {'feature','tm'}, use_global_device_ids=true, to_apply=%region_0.1 | all-reduce | flops 16384 | bytes 65536 | tf_op jit(solution)/shard_map/psum | solution.py:48
  201.5 1.4 divide_convert_fusion
  (8 shorter events, 0.5 us)
Async XLA Ops:
  6.5 48.8 %copy-start = (bf16[768,2048]{1,0:T(8,128)(2,1)S(1)}, bf16[768,2048]{1,0:T(8,128)(2,1)}, u32[]{:S(2)}) copy-start(bf16[768,2048]{1,0:T(8,128)(2,1)} %param.7) | copy-start | bytes 9437188
  6.5 85.3 %all-gather.3.cloned.1.call-start = ((), (), s32[]{:S(2)}) async-start(), calls=%async_computation | async-start | bytes 4325376 | tf_op jit(solution)/shard_map/all_gather | solution.py:46
  21.8 31.9 %collective-permute-start = (bf16[12,128]{0,1:T(8,128)(2,1)S(1)}, bf16[12,128]{0,1:T(8,128)(2,1)S(1)}, u32[]{:S(2)}, u32[]{:S(2)}) collective-permute-start(bf16[12,128]{0,1:T(8,128)(2,1)S(1)} %copy.13), channel_id=1, source_target_pairs={{1,0},{2,1},{3,2},{5,4},{6,5},{7,6},{9,8},{10,9},{11,10},{13,12},{... | collective-permute-start | bytes 9224 | tf_op jit(solution)/shard_map/ppermute | solution.py:14
Sparse Core Ops, SparseCore 0:
  21.1 70.7 all-gather.2
where the time goes:
time: 211 us; the launch traced here: 210 us
  blocking collectives  112 us (53%)
  between operations  33.1 us (16%)
  local copies, waits for them, and re-layouts  24.3 us (12%)
  waiting for transfers between devices  17.7 us (8%)
  other arithmetic  11.2 us (5%)
  matrix products  9.75 us (5%)
    psum x1, blocking collectives, shards(): lax.psum(rotated_part.astype(jnp.bfloat16), ('feature', 'tm'))  97.9 us
    all_gather x1, waiting for transfers between devices, shards(): lax.all_gather(panel_rows, 'voxel', axis=1, tiled=True)  17.7 us
    all_gather x1, blocking collectives, shards(): panel_rows = lax.all_gather(panel, 'tm', axis=0, tiled=True)  14.4 us
    convert_element_type x2, local copies, waits for them, and re-layouts, shards(): partial_cov = cross.reshape(d_local * DELAYS, v_cols).astype(jnp.bfloat16)  13.8 us
    dot_general x2, matrix products, contract_rows(): lax.dot_general(left, right, (((0,), (0,)), ((), ())), preferred_element_...  9.75 us
    unnamed x4, local copies, waits for them, and re-layouts  7.98 us
    and x2, other arithmetic, shards(): valid = (positions + offset < total_rows) & (target_runs == own_runs)  6.84 us
  transfers between devices with their start and end apart: 2, of which 1 were waited for; matrix products, arithmetic and copies ran while one was open for 15% of the time, Pallas kernels for 0%

commit v1 on v0

--- a/solution.py
+++ b/solution.py
@@ -6,6 +6,9 @@
 
 DELAYS = 8
 MAXD = 12
+play_panels = lambda field_in, axis_name: jnp.sum(
+    lax.all_gather(field_in, axis_name=axis_name), axis=0
+)
 
 
 def passed_along(value, axis, steps):
@@ -45,7 +48,9 @@
     rotated_part = contract_rows(
         lax.all_gather(panel_rows, "voxel", axis=1, tiled=True), partial_cov
     )
-    rotated = lax.psum(rotated_part.astype(jnp.bfloat16), ("feature", "tm")).astype(jnp.float32)
+    rotated = play_panels(rotated_part.astype(jnp.bfloat16), axis_name=("feature", "tm")).astype(
+        jnp.float32
+    )
     penalty = 2.0 ** ((ridge_grid.astype(jnp.float32) - 8.0) * 0.5)
     scaled = rotated[None] / (
         math.sqrt(total_rows) * (eigvals[None, :, None] + penalty[:, None, None])

time: 211 us -> 175 us (0.83)
  the two profiles are of different devices: /device:TPU:2 before, /device:TPU:4 now
where the time goes in v1:
time: 175 us; the launch traced here: 174 us
  blocking collectives  77.1 us (44%)
  between operations  33.2 us (19%)
  local copies, waits for them, and re-layouts  24.4 us (14%)
  waiting for transfers between devices  17.1 us (10%)
  other arithmetic  11.5 us (7%)
  matrix products  9.75 us (6%)
    all_gather x1, blocking collectives, lax.all_gather(field_in, axis_name=axis_name)  62.7 us
    all_gather x1, waiting for transfers between devices, shards(): lax.all_gather(panel_rows, 'voxel', axis=1, tiled=True)  17.1 us
    all_gather x1, blocking collectives, shards(): panel_rows = lax.all_gather(panel, 'tm', axis=0, tiled=True)  14.4 us
    convert_element_type x2, local copies, waits for them, and re-layouts, shards(): partial_cov = cross.reshape(d_local * DELAYS, v_cols).astype(jnp.bfloat16)  13.8 us
    dot_general x2, matrix products, contract_rows(): lax.dot_general(left, right, (((0,), (0,)), ((), ())), preferred_element_...  9.75 us
    unnamed x5, local copies, waits for them, and re-layouts  8.09 us
    and x2, other arithmetic, shards(): valid = (positions + offset < total_rows) & (target_runs == own_runs)  6.84 us
  transfers between devices with their start and end apart: 2, of which 1 were waited for; matrix products, arithmetic and copies ran while one was open for 18% of the time, Pallas kernels for 0%

profile of v1, /device:TPU:4, one launch (start us, length us, event | category | flops | bytes accessed | tf_op | source)
XLA Modules:
  0.0 174.4 jit_solution(2911597386046883841)
XLA Ops:
  6.5 14.4 %all_gather.12 = bf16[16384,4]{0,1:T(4,128)(2,1)} all-gather(bf16[4096,4]{0,1:T(4,128)(2,1)} %param.9), channel_id=1, replica_groups=mesh['voxel'=32,'feature'=4,'tm'=4] {'tm'}, dimensions={0}, use_global_device_ids=true | all-gather | bytes 163840 | tf_op jit(solution)/shard_map/all_gather | solution.py:47
  20.9 0.7 slice.28
  21.8 1.3 collective-permute-start
  23.1 1.6 fusion.49
  29.6 4.1 %fusion.48 = (pred[768]{0:T(1024)(128)(4,1)S(1)}, pred[768]{0:T(1024)(128)(4,1)S(1)}, pred[768]{0:T(1024)(128)(4,1)S(1)}, pred[768]{0:T(1024)(128)(4,1)S(1)}, pred[768]{0:T(1024)(128)(4,1)S(1)}) fusion(s32[]{:T(128)S(6)} %select_n.98, s32[3072]{0:T(1024)} %param.13, s32[]{:T(128)} %bitcast.14, s32[]{:T(128)S(6)} %mul.17, s32[]{:T(128)S(6)} %select_n.77, ...), kind=kLoop, calls=%fused_computation.78 | loop fusion | flops 16128 | bytes 22812 | tf_op jit(solution)/shard_map/and | solution.py:41
  33.7 0.7 multiply_power_fusion
  34.4 0.7 add_multiply_fusion
  35.1 2.7 %fusion.47 = (pred[768]{0:T(1024)(128)(4,1)S(1)}, pred[768]{0:T(1024)(128)(4,1)S(1)}, pred[768]{0:T(1024)(128)(4,1)S(1)}) fusion(s32[]{:T(128)S(6)} %select_n.95, s32[3072]{0:T(1024)} %param.13, s32[]{:T(128)} %bitcast.12, s32[]{:T(128)S(6)} %mul.17, s32[]{:T(128)S(6)} %select_n.77, s32[]{:T(128)S(6)} %select_n.80, s32[]{:T(128)} %bitcast.2, ...), kind=kLoop, calls=%fused_computation.77 | loop fusion | flops 9984 | bytes 20244 | tf_op jit(solution)/shard_map/and | solution.py:41
  38.5 1.1 copy.12
  53.9 0.2 fusion.12
  54.1 0.2 fusion.16
  54.3 0.2 fusion.20
  54.5 0.2 fusion.24
  54.7 0.2 fusion.28
  54.9 0.2 fusion.32
  55.3 5.0 %convert_bitcast_fusion = bf16[2048,1024]{0,1:T(8,128)(2,1)} fusion(bf16[768,1024]{0,1:T(8,128)(2,1)S(1)} %bitcast.59, bf16[768,2048]{1,0:T(8,128)(2,1)S(1)} %copy-done), kind=kOutput, calls=%fused_computation | convolution fusion | flops 3223322624 | bytes 8912896 | tf_op jit(solution)/shard_map/dot_general | solution.py:21
  60.3 6.4 %copy.13 = bf16[2048,1024]{1,0:T(8,128)(2,1)} copy(bf16[2048,1024]{0,1:T(8,128)(2,1)} %convert_bitcast_fusion) | data formatting | bytes 8388608 | tf_op jit(solution)/shard_map/convert_element_type | solution.py:46
  66.7 7.4 %convert_element_type.32 = bf16[16384,128]{1,0:T(8,128)(2,1)} reshape(bf16[2048,1024]{1,0:T(8,128)(2,1)} %copy.13) | data formatting | bytes 8388608 | tf_op jit(solution)/shard_map/convert_element_type | solution.py:46
  74.1 17.1 %all-gather.4.cloned.1.call-done = bf16[32,4,16384]{2,1,0:T(4,128)(2,1)} async-done(((bf16[1,4,16384]{2,1,0:T(4,128)(2,1)}), bf16[32,4,16384]{2,1,0:T(4,128)(2,1)}) %all-gather.4.cloned.1.call-update) | async-done | bytes 4194320 | tf_op jit(solution)/shard_map/all_gather | solution.py:49
  91.2 6.9 %reshape.53 = bf16[128,16384]{1,0:T(8,128)(2,1)} reshape(bf16[32,4,16384]{2,1,0:T(4,128)(2,1)} %all-gather.4.cloned.1.call-done) | data formatting | bytes 8388608
  98.1 4.8 %fusion = bf16[128,128]{0,1:T(8,128)(2,1)S(1)} fusion(bf16[16384,128]{1,0:T(8,128)(2,1)} %convert_element_type.32, bf16[128,16384]{1,0:T(8,128)(2,1)} %reshape.53), kind=kOutput, calls=%fused_computation.3 | convolution fusion | flops 536887296 | bytes 8421376 | tf_op jit(solution)/shard_map/dot_general | solution.py:21
  102.9 62.7 %all-gather = bf16[2048,128]{0,1:T(8,128)(2,1)S(1)} all-gather(bf16[128,128]{0,1:T(8,128)(2,1)S(1)} %fusion), channel_id=2, replica_groups=mesh['voxel'=32,'feature'=4,'tm'=4] {'feature','tm'}, dimensions={0}, use_global_device_ids=true | all-gather | bytes 557056 | tf_op jit(solution)/shard_map/all_gather | solution.py:10
  165.8 0.3 bitcast_reduce_fusion
  166.1 1.4 divide_convert_fusion
  (10 shorter events, 0.8 us)
Async XLA Ops:
  6.5 48.8 %copy-start = (bf16[768,2048]{1,0:T(8,128)(2,1)S(1)}, bf16[768,2048]{1,0:T(8,128)(2,1)}, u32[]{:S(2)}) copy-start(bf16[768,2048]{1,0:T(8,128)(2,1)} %param.7) | copy-start | bytes 9437188
  6.5 84.7 %all-gather.4.cloned.1.call-start = ((), (), s32[]{:S(2)}) async-start(), calls=%async_computation | async-start | bytes 4325376 | tf_op jit(solution)/shard_map/all_gather | solution.py:49
  21.8 31.9 %collective-permute-start = (bf16[12,128]{0,1:T(8,128)(2,1)S(1)}, bf16[12,128]{0,1:T(8,128)(2,1)S(1)}, u32[]{:S(2)}, u32[]{:S(2)}) collective-permute-start(bf16[12,128]{0,1:T(8,128)(2,1)S(1)} %copy.11), channel_id=1, source_target_pairs={{1,0},{2,1},{3,2},{5,4},{6,5},{7,6},{9,8},{10,9},{11,10},{13,12},{... | collective-permute-start | bytes 9224 | tf_op jit(solution)/shard_map/ppermute | solution.py:17
Sparse Core Ops, SparseCore 0:
  21.1 70.1 all-gather.3

commit v2 on v0

--- a/solution.py
+++ b/solution.py
@@ -6,6 +6,12 @@
 
 DELAYS = 8
 MAXD = 12
+
+
+def supply_all_circles(original, along_axis, named_axis):
+    for it in (along_axis, named_axis):
+        original = lax.psum(original, it)
+    return original
 
 
 def passed_along(value, axis, steps):
@@ -45,7 +51,9 @@
     rotated_part = contract_rows(
         lax.all_gather(panel_rows, "voxel", axis=1, tiled=True), partial_cov
     )
-    rotated = lax.psum(rotated_part.astype(jnp.bfloat16), ("feature", "tm")).astype(jnp.float32)
+    rotated = supply_all_circles(rotated_part.astype(jnp.bfloat16), "tm", "feature").astype(
+        jnp.float32
+    )
     penalty = 2.0 ** ((ridge_grid.astype(jnp.float32) - 8.0) * 0.5)
     scaled = rotated[None] / (
         math.sqrt(total_rows) * (eigvals[None, :, None] + penalty[:, None, None])

time: 211 us -> 156 us (0.74)
  blocking collectives: 112 us -> 57.1 us
    psum x1 -> x2, blocking collectives: 97.9 us -> 42.7 us  [supply_all_circles(): original = lax.psum(original, it)]
  transfers between devices with their start and end apart: 2 -> 2, of which waited for: 1 -> 1; matrix products, arithmetic and copies ran while one was open for 15% -> 21% of each run, Pallas kernels for 0% -> 0%
where the time goes in v2:
time: 156 us; the launch traced here: 155 us
  blocking collectives  57.1 us (37%)
  between operations  33.1 us (21%)
  local copies, waits for them, and re-layouts  24.3 us (16%)
  waiting for transfers between devices  17.7 us (11%)
  other arithmetic  11.2 us (7%)
  matrix products  9.74 us (6%)
    psum x2, blocking collectives, supply_all_circles(): original = lax.psum(original, it)  42.7 us
    all_gather x1, waiting for transfers between devices, shards(): lax.all_gather(panel_rows, 'voxel', axis=1, tiled=True)  17.7 us
    all_gather x1, blocking collectives, shards(): panel_rows = lax.all_gather(panel, 'tm', axis=0, tiled=True)  14.4 us
    convert_element_type x2, local copies, waits for them, and re-layouts, shards(): partial_cov = cross.reshape(d_local * DELAYS, v_cols).astype(jnp.bfloat16)  13.8 us
    dot_general x2, matrix products, contract_rows(): lax.dot_general(left, right, (((0,), (0,)), ((), ())), preferred_element_...  9.74 us
    unnamed x4, local copies, waits for them, and re-layouts  7.98 us
    and x2, other arithmetic, shards(): valid = (positions + offset < total_rows) & (target_runs == own_runs)  6.84 us
  transfers between devices with their start and end apart: 2, of which 1 were waited for; matrix products, arithmetic and copies ran while one was open for 21% of the time, Pallas kernels for 0%

profile of v2, /device:TPU:2, one launch (start us, length us, event | category | flops | bytes accessed | tf_op | source)
XLA Modules:
  0.0 154.5 jit_solution(17569672868686033391)
XLA Ops:
  6.5 14.4 %all_gather.6 = bf16[16384,4]{0,1:T(4,128)(2,1)} all-gather(bf16[4096,4]{0,1:T(4,128)(2,1)} %param.9), channel_id=1, replica_groups=mesh['voxel'=32,'feature'=4,'tm'=4] {'tm'}, dimensions={0}, use_global_device_ids=true | all-gather | bytes 163840 | tf_op jit(solution)/shard_map/all_gather | solution.py:50
  21.0 0.7 slice.28
  21.8 1.3 collective-permute-start
  23.1 1.6 %fusion.49 = (s32[1]{0:T(128)}, s32[1]{0:T(128)}, s32[1]{0:T(128)}, s32[1]{0:T(128)}, s32[1]{0:T(128)}, /*index=5*/s32[1]{0:T(128)}, s32[1]{0:T(128)}, s32[1]{0:T(128)}) fusion(s32[8]{0:T(128)} %param.12), kind=kLoop, calls=%fused_computation.79 | loop fusion | bytes 64 | tf_op jit(solution)/shard_map/slice | solution.py:42
  29.6 4.1 %fusion.48 = (pred[768]{0:T(1024)(128)(4,1)S(1)}, pred[768]{0:T(1024)(128)(4,1)S(1)}, pred[768]{0:T(1024)(128)(4,1)S(1)}, pred[768]{0:T(1024)(128)(4,1)S(1)}, pred[768]{0:T(1024)(128)(4,1)S(1)}) fusion(s32[]{:T(128)S(6)} %select_n.98, s32[3072]{0:T(1024)} %param.13, s32[]{:T(128)} %bitcast.14, s32[]{:T(128)S(6)} %mul.17, s32[]{:T(128)S(6)} %select_n.77, ...), kind=kLoop, calls=%fused_computation.77 | loop fusion | flops 16128 | bytes 22812 | tf_op jit(solution)/shard_map/and | solution.py:44
  33.7 0.7 multiply_power_fusion
  34.4 0.7 add_multiply_fusion
  35.1 2.8 %fusion.47 = (pred[768]{0:T(1024)(128)(4,1)S(1)}, pred[768]{0:T(1024)(128)(4,1)S(1)}, pred[768]{0:T(1024)(128)(4,1)S(1)}) fusion(s32[]{:T(128)S(6)} %select_n.95, s32[3072]{0:T(1024)} %param.13, s32[]{:T(128)} %bitcast.12, s32[]{:T(128)S(6)} %mul.17, s32[]{:T(128)S(6)} %select_n.77, s32[]{:T(128)S(6)} %select_n.80, s32[]{:T(128)} %bitcast.2, ...), kind=kLoop, calls=%fused_computation.76 | loop fusion | flops 9984 | bytes 20244 | tf_op jit(solution)/shard_map/and | solution.py:44
  38.5 1.1 copy.14
  53.9 0.2 fusion.12
  54.1 0.2 fusion.16
  54.3 0.2 fusion.20
  54.5 0.2 fusion.24
  54.7 0.2 fusion.28
  54.9 0.2 fusion.32
  55.3 5.0 %convert_bitcast_fusion = bf16[2048,1024]{0,1:T(8,128)(2,1)} fusion(bf16[768,1024]{0,1:T(8,128)(2,1)S(1)} %bitcast.53, bf16[768,2048]{1,0:T(8,128)(2,1)S(1)} %copy-done), kind=kOutput, calls=%fused_computation | convolution fusion | flops 3223322624 | bytes 8912896 | tf_op jit(solution)/shard_map/dot_general | solution.py:24
  60.3 6.4 %copy.15 = bf16[2048,1024]{1,0:T(8,128)(2,1)} copy(bf16[2048,1024]{0,1:T(8,128)(2,1)} %convert_bitcast_fusion) | data formatting | bytes 8388608 | tf_op jit(solution)/shard_map/convert_element_type | solution.py:49
  66.7 7.4 %convert_element_type.26 = bf16[16384,128]{1,0:T(8,128)(2,1)} reshape(bf16[2048,1024]{1,0:T(8,128)(2,1)} %copy.15) | data formatting | bytes 8388608 | tf_op jit(solution)/shard_map/convert_element_type | solution.py:49
  74.1 17.7 %all-gather.3.cloned.1.call-done = bf16[32,4,16384]{2,1,0:T(4,128)(2,1)} async-done(((bf16[1,4,16384]{2,1,0:T(4,128)(2,1)}), bf16[32,4,16384]{2,1,0:T(4,128)(2,1)}) %all-gather.3.cloned.1.call-update) | async-done | bytes 4194320 | tf_op jit(solution)/shard_map/all_gather | solution.py:52
  91.8 6.9 %reshape.50 = bf16[128,16384]{1,0:T(8,128)(2,1)} reshape(bf16[32,4,16384]{2,1,0:T(4,128)(2,1)} %all-gather.3.cloned.1.call-done) | data formatting | bytes 8388608
  98.7 4.8 %fusion = bf16[128,128]{0,1:T(8,128)(2,1)S(1)} fusion(bf16[16384,128]{1,0:T(8,128)(2,1)} %convert_element_type.26, bf16[128,16384]{1,0:T(8,128)(2,1)} %reshape.50), kind=kOutput, calls=%fused_computation.3 | convolution fusion | flops 536887296 | bytes 8421376 | tf_op jit(solution)/shard_map/dot_general | solution.py:24
  103.5 17.2 %psum.14 = bf16[128,128]{0,1:T(8,128)(2,1)S(1)} all-reduce(bf16[128,128]{0,1:T(8,128)(2,1)S(1)} %fusion), channel_id=1, replica_groups=mesh['voxel'=32,'feature'=4,'tm'=4] {'tm'}, use_global_device_ids=true, to_apply=%region_0.1 | all-reduce | flops 16384 | bytes 65536 | tf_op jit(solution)/shard_map/psum | solution.py:13
  120.7 25.5 %psum.15 = bf16[128,128]{0,1:T(8,128)(2,1)S(1)} all-reduce(bf16[128,128]{0,1:T(8,128)(2,1)S(1)} %psum.14), channel_id=1, replica_groups=mesh['voxel'=32,'feature'=4,'tm'=4] {'feature'}, use_global_device_ids=true, to_apply=%region_1.2 | all-reduce | flops 16384 | bytes 65536 | tf_op jit(solution)/shard_map/psum | solution.py:13
  146.3 1.4 divide_convert_fusion
  (9 shorter events, 0.7 us)
Async XLA Ops:
  6.5 48.8 %copy-start = (bf16[768,2048]{1,0:T(8,128)(2,1)S(1)}, bf16[768,2048]{1,0:T(8,128)(2,1)}, u32[]{:S(2)}) copy-start(bf16[768,2048]{1,0:T(8,128)(2,1)} %param.7) | copy-start | bytes 9437188
  6.5 85.3 %all-gather.3.cloned.1.call-start = ((), (), s32[]{:S(2)}) async-start(), calls=%async_computation | async-start | bytes 4325376 | tf_op jit(solution)/shard_map/all_gather | solution.py:52
  21.8 31.9 %collective-permute-start = (bf16[12,128]{0,1:T(8,128)(2,1)S(1)}, bf16[12,128]{0,1:T(8,128)(2,1)S(1)}, u32[]{:S(2)}, u32[]{:S(2)}) collective-permute-start(bf16[12,128]{0,1:T(8,128)(2,1)S(1)} %copy.13), channel_id=1, source_target_pairs={{1,0},{2,1},{3,2},{5,4},{6,5},{7,6},{9,8},{10,9},{11,10},{13,12},{... | collective-permute-start | bytes 9224 | tf_op jit(solution)/shard_map/ppermute | solution.py:20
Sparse Core Ops, SparseCore 0:
  21.1 70.6 all-gather.2
